TPU v7x, 32 devices: a whole 2x2x4 slice. The times are simulated.
32 devices in a mesh: dp: 8 (over z, x), head: 4 (over y, core).
Axes of the slice: x: 2, y: 2, z: 4, core: 2. Of those that a mesh axis runs over, the one named last changes fastest.
Arguments:
- residual: bfloat16 [32, 4096], P('dp', 'head'), may hold values from -6 to 6
- query: bfloat16 [32, 32, 128], P('dp', 'head'), may hold values from -4.5 to 4.5
- fresh_token_keys: bfloat16 [32, 8, 128], P('dp', 'head'), may hold values from -4.5 to 4.5
- value_new: bfloat16 [32, 8, 128], P('dp', 'head'), may hold values from -24 to 24
- key_cache: bfloat16 [32, 8, 2048, 128], P('dp', 'head'), may hold values from -6 to 6
- value_cache: bfloat16 [32, 8, 2048, 128], P('dp', 'head'), may hold values from -6 to 6
- lengths: int32 [32], P('dp'), may hold values from 1024 to 2048, as said below
- pages: int32 [32, 8, 64], P('dp', 'head'), may hold values from 0 to 127, as said below
- w_out: bfloat16 [4096, 4096], P('head', 'dp'), may hold values from -0.75 to 0.75
- norm_gain: float32 [4096], P('head'), may hold values from 0.5 to 1.5
- expert_ids: int32 [32, 2], P('dp'), may hold values from 0 to 7, all different within a row; in each aligned block of 4 rows (0 to 3, 4 to 7, ...) at most 2 rows name the same one
- gate_weights: float32 [32, 2], P('dp'), may hold values from 0.1 to 1
- w_in: bfloat16 [8, 2, 4096, 7168], P('dp', None, None, 'head'), may hold values from -0.09375 to 0.09375
- w_down: bfloat16 [8, 7168, 4096], P('dp', 'head'), may hold values from -0.0625 to 0.0625
Outputs:
- layer_out: bfloat16 [32, 4096], P('dp', 'head')
Inputs may be any that keep to these rules, and one draw needn't show every extreme that they name: `lengths`: each request's length; some request has exactly 2048 and some exactly 1024. `pages`: for each request and key head, 64 distinct page numbers, all below ceil(length / 16), always including the page that holds the request's last cached token; in no fixed order. `expert_ids`: per token 2 distinct experts; among the 4 tokens of one dp index no expert is named more than 2 times.
All inputs are finite; a program needn't handle non-finite values.
Results may differ from a plain program's by a relative error of at most 0.012.
Values may be sent and summed in bfloat16 or wider, within the bound.
A program may use at most 128 MiB of HBM per device.

v0:
```python
import jax
import jax.numpy as jnp
from jax import lax
from jax.sharding import PartitionSpec as P

EXPERTS = 8
TOP = 2
PAGE = 16
MOST = 2
EPSILON = 1e-05


def shards(
    residual,
    query,
    fresh_token_keys,
    value_new,
    key_cache,
    value_cache,
    lengths,
    pages,
    w_out,
    norm_gain,
    expert_ids,
    gate_weights,
    w_in,
    w_down,
):
    tok_rows = query.shape[0]
    head_local = query.shape[1]
    head_dim = query.shape[2]
    kv_local = key_cache.shape[1]
    cache_len = key_cache.shape[2]
    page_total = cache_len // PAGE
    group_member_count = head_local // kv_local
    page_numbers = jnp.arange(page_total, dtype=jnp.int32)
    page_chosen = jnp.any(pages[:, :, :, None] == page_numbers[None, None, None, :], axis=2)
    position_chosen = jnp.broadcast_to(
        page_chosen[:, :, :, None], (tok_rows, kv_local, page_total, PAGE)
    ).reshape(tok_rows, kv_local, cache_len)
    position_ids = jnp.arange(cache_len, dtype=jnp.int32)
    in_range = (position_chosen & (position_ids[None, None, :] < lengths[:, None, None]))[
        :, :, None, :
    ]
    grouped_rows = query.reshape(tok_rows, kv_local, group_member_count, head_dim)
    score_scale = head_dim ** (-0.5)
    scores = (
        jnp.einsum("bkgd,bksd->bkgs", grouped_rows, key_cache, preferred_element_type=jnp.float32)
        * score_scale
    )
    own_score = (
        jnp.einsum(
            "luxe,lue->lux", grouped_rows, fresh_token_keys, preferred_element_type=jnp.float32
        )
        * score_scale
    )
    masked = jnp.where(in_range, scores, -1e30)
    row_top = jnp.maximum(jnp.max(masked, axis=-1), own_score)
    expo = jnp.where(in_range, jnp.exp(scores - row_top[..., None]), 0.0)
    own_expo = jnp.exp(own_score - row_top)
    denominator = jnp.sum(expo, axis=-1) + own_expo
    weights = (expo / denominator[..., None]).astype(jnp.bfloat16)
    own_weight = (own_expo / denominator).astype(jnp.bfloat16)
    attended = jnp.einsum(
        "bkgs,bksd->bkgd", weights, value_cache, preferred_element_type=jnp.float32
    )
    attended = (
        attended
        + own_weight.astype(jnp.float32)[..., None] * value_new.astype(jnp.float32)[:, :, None, :]
    )
    attn_rows = attended.reshape(tok_rows, head_local * head_dim).astype(jnp.bfloat16)
    every_row = lax.all_gather(attn_rows, "dp", axis=0, tiled=True)
    column_part = jnp.dot(every_row, w_out, preferred_element_type=jnp.float32)
    head_partial = lax.all_to_all(
        column_part.astype(jnp.bfloat16), "dp", split_axis=0, concat_axis=1, tiled=True
    ).astype(column_part.dtype)
    stream = residual.astype(jnp.float32) + lax.psum_scatter(
        head_partial.astype(jnp.bfloat16), "head", scatter_dimension=1, tiled=True
    ).astype(jnp.float32)
    whole_stream, whole_gain = (
        lax.all_gather(stream, "head", axis=1, tiled=True),
        lax.all_gather(norm_gain, "head", axis=0, tiled=True),
    )
    square_mean_value = jnp.mean(whole_stream * whole_stream, axis=-1)
    normed = (
        whole_stream * lax.rsqrt(square_mean_value + EPSILON)[:, None] * whole_gain[None, :]
    ).astype(jnp.bfloat16)
    group_count = lax.axis_size("dp") // EXPERTS
    assignments = tok_rows * TOP
    flat_ids = expert_ids.reshape(assignments)
    expert_range = jnp.arange(EXPERTS, dtype=jnp.int32)
    onehot = (flat_ids[:, None] == expert_range[None, :]).astype(jnp.int32)
    earlier = jnp.cumsum(onehot, axis=0) - onehot
    slot_index = jnp.sum(earlier * onehot, axis=1)
    target = flat_ids * MOST + slot_index
    placement_map = jnp.arange(EXPERTS * MOST, dtype=jnp.int32)[:, None] == target[None, :]
    token_map = jnp.any(placement_map.reshape(EXPERTS * MOST, tok_rows, TOP), axis=2)
    outgoing = jnp.dot(
        token_map.astype(jnp.bfloat16), normed, preferred_element_type=jnp.float32
    ).astype(jnp.bfloat16)
    width_of_row = outgoing.shape[1]
    outgoing = jnp.broadcast_to(
        outgoing.reshape(EXPERTS, 1, MOST, width_of_row), (EXPERTS, group_count, MOST, width_of_row)
    )
    outgoing = outgoing.reshape(EXPERTS * group_count, MOST, width_of_row)
    arrived = lax.all_to_all(outgoing, "dp", split_axis=0, concat_axis=0, tiled=True)
    senders, slot_count, feature_count = arrived.shape
    flat_rows = arrived.reshape(senders * slot_count, feature_count)
    gate_act = jnp.dot(flat_rows, w_in[0, 0], preferred_element_type=jnp.float32)
    up_act = jnp.dot(flat_rows, w_in[0, 1], preferred_element_type=jnp.float32)
    hidden = (jax.nn.silu(gate_act) * up_act).astype(jnp.bfloat16)
    slab_out = jnp.dot(hidden, w_down[0], preferred_element_type=jnp.float32).reshape(
        senders, slot_count, w_down.shape[2]
    )
    summed_total = lax.psum_scatter(
        slab_out.astype(jnp.bfloat16), "head", scatter_dimension=2, tiled=True
    ).astype(jnp.float32)
    returned = lax.all_to_all(
        summed_total.astype(jnp.bfloat16), "dp", split_axis=0, concat_axis=0, tiled=True
    ).astype(summed_total.dtype)
    local_width = returned.shape[2]
    per_expert = jnp.sum(returned.reshape(EXPERTS, group_count, MOST, local_width), axis=1).reshape(
        EXPERTS * MOST, local_width
    )
    weighted = jnp.where(placement_map, gate_weights.reshape(assignments)[None, :], 0.0)
    combine_map = jnp.sum(weighted.reshape(EXPERTS * MOST, tok_rows, TOP), axis=2)
    mixture = jnp.dot(
        combine_map.T,
        per_expert,
        precision=lax.Precision.HIGHEST,
        preferred_element_type=jnp.float32,
    )
    return (stream + mixture).astype(jnp.bfloat16)


def solution(mesh):
    in_specs = (
        P("dp", "head"),
        P("dp", "head", None),
        P("dp", "head", None),
        P("dp", "head", None),
        P("dp", "head", None, None),
        P("dp", "head", None, None),
        P("dp"),
        P("dp", "head", None),
        P("head", "dp"),
        P("head"),
        P("dp", None),
        P("dp", None),
        P("dp", None, None, "head"),
        P("dp", "head", None),
    )
    out_specs = P("dp", "head")
    return jax.shard_map(shards, mesh=mesh, in_specs=in_specs, out_specs=out_specs, check_vma=False)
```

profile of v0, /device:TPU:0, one launch (start us, length us, event | category | flops | bytes accessed | tf_op | source)
XLA Modules:
  0.0 169.4 jit_solution(6646213300250157299)
XLA Ops:
  6.5 0.9 fusion.19
  8.0 0.7 iota_compare_fusion.1
  8.8 0.8 fusion.30
  9.6 3.5 %select_reduce_fusion = (f32[4,2,4]{2,1,0:T(2,128)S(1)}, f32[4,2,4,2048]{3,2,1,0:T(4,128)S(1)}) fusion(pred[4,2,2048]{2,1,0:T(4,128)(4,1)S(1)} %copy.32, bf16[4,2,4,128]{3,2,1,0:T(4,128)(2,1)} %bitcast.52, bf16[4,2,2048,128]{3,2,1,0:T(8,128)(2,1)} %param.18), kind=kOutput, calls=%fused_computation.19 | convolution fusion | flops 16973792 | bytes 4481152 | tf_op jit(solution)/shard_map/bkgd,bksd->bkgs/dot_general | solution.py:48
  13.5 0.7 convert_element_type.55
  14.1 2.9 %fusion.18 = bf16[4,2,4,128]{3,2,1,0:T(4,128)(2,1)S(1)} fusion(bf16[4,2,2048,128]{3,2,1,0:T(8,128)(2,1)} %param.19, f32[4,2,4,2048]{3,2,1,0:T(4,128)S(1)} %get-tuple-element.8, f32[4,2,4]{2,1,0:T(2,128)S(1)} %get-tuple-element.6, f32[4,2,4]{2,1,0:T(2,128)S(1)} %multiply_maximum_fusion, pred[4,2,2048]{2,1,0:T(4,128)(4,1)S(1)} %copy.32, ...), kind=kOutput, calls=%fused_computation.17 | convolution fusion | flops 17051648 | bytes 4485504 | tf_op jit(solution)/shard_map/bkgs,bksd->bkgd/dot_general | solution.py:64
  17.1 32.4 %all-gather = bf16[8,4,1024]{2,1,0:T(4,128)(2,1)S(1)} all-gather(bf16[1,4,1024]{2,1,0:T(4,128)(2,1)S(1)} %reshape.99), channel_id=1, replica_groups=mesh['dp'=8,'head'=4] {'dp'}, dimensions={0}, use_global_device_ids=true | all-gather | bytes 73728 | tf_op jit(solution)/shard_map/all_gather | solution.py:72
  50.4 5.5 %all-to-all-start = ((bf16[8,4,512]{2,1,0:T(4,128)(2,1)}), bf16[8,4,512]{2,1,0:T(4,128)(2,1)S(1)}, u32[]{:S(2)}, u32[]{:S(2)}) async-start(bf16[8,4,512]{2,1,0:T(4,128)(2,1)} %all_to_all.20), calls=%async_computation | async-start | bytes 65536 | tf_op jit(solution)/shard_map/all_to_all | solution.py:74
  55.9 0.8 copy.33
  57.2 5.3 %all_gather.11 = f32[4096]{0:T(1024)S(1)} all-gather(f32[1024]{0:T(1024)} %param.23), channel_id=1, replica_groups=mesh['dp'=8,'head'=4] {'head'}, dimensions={0}, use_global_device_ids=true | all-gather | bytes 20480 | tf_op jit(solution)/shard_map/all_gather | solution.py:82
  62.6 1.4 copy.40
  64.1 26.2 %reduce-scatter.7.cloned.1.call-done = bf16[1024,4]{1,0:T(8,128)(2,1)} async-done(((bf16[4096,4]{1,0:T(8,128)(2,1)}), bf16[1024,4]{1,0:T(8,128)(2,1)}) %reduce-scatter.7.cloned.1.call-update) | async-done | bytes 8208
  90.3 1.1 copy.41
  91.4 0.7 convert_add_fusion
  92.1 5.2 %all_gather.10 = f32[4,4096]{1,0:T(4,128)S(1)} all-gather(f32[4,1024]{1,0:T(4,128)S(1)} %convert_add_fusion), channel_id=1, replica_groups=mesh['dp'=8,'head'=4] {'head'}, dimensions={1}, use_global_device_ids=true | all-gather | bytes 81920 | tf_op jit(solution)/shard_map/all_gather | solution.py:81
  97.8 12.8 %all_to_all.29 = bf16[8,2,4096]{2,1,0:T(2,128)(2,1)S(1)} all-to-all(bf16[8,2,4096]{2,1,0:T(2,128)(2,1)S(1)} %reshape_reshape.3), channel_id=1, replica_groups=mesh['dp'=8,'head'=4] {'dp'}, dimensions={0} | all-to-all | bytes 262144 | tf_op jit(solution)/shard_map/all_to_all | solution.py:106
  110.7 6.2 %fusion.4 = f32[16,1792]{1,0:T(8,128)S(1)} fusion(bf16[16,4096]{1,0:T(8,128)(2,1)S(1)} %reshape.97, bf16[1,2,4096,1792]{3,2,1,0:T(8,128)(2,1)} %param.26), kind=kOutput, calls=%fused_computation.4 | convolution fusion | flops 234881024 | bytes 14925824 | tf_op jit(solution)/shard_map/dot_general | solution.py:109
  117.0 6.3 %fusion.14 = bf16[16,1792]{1,0:T(8,128)(2,1)S(1)} fusion(bf16[16,4096]{1,0:T(8,128)(2,1)S(1)} %reshape.97, bf16[1,2,4096,1792]{3,2,1,0:T(8,128)(2,1)} %param.26, f32[16,1792]{1,0:T(8,128)S(1)} %fusion.4), kind=kOutput, calls=%fused_computation.12 | convolution fusion | flops 235053056 | bytes 14983168 | tf_op jit(solution)/shard_map/dot_general | solution.py:110
  123.3 7.8 %fusion.8 = bf16[8,2,4096]{2,0,1:T(8,128)(2,1)} fusion(bf16[1,1792,4096]{2,1,0:T(8,128)(2,1)} %param.27, bf16[8,2,1792]{2,1,0:T(2,128)(2,1)S(1)} %dot_general.36), kind=kOutput, calls=%fused_computation.8 | convolution fusion | flops 234946560 | bytes 14868480 | tf_op jit(solution)/shard_map/dot_general | solution.py:112
  131.2 17.0 %reduce-scatter.5.cloned.1.call-done = bf16[8,2,1024]{2,0,1:T(8,128)(2,1)} async-done(((bf16[8,2,4096]{2,0,1:T(8,128)(2,1)}), bf16[8,2,1024]{2,0,1:T(8,128)(2,1)}) %reduce-scatter.5.cloned.1.call-update) | async-done | bytes 32784 | tf_op jit(solution)/shard_map/reduce_scatter | solution.py:115
  148.2 1.4 copy.37
  149.6 5.5 %all-to-all-start.2 = ((bf16[8,2,1024]{2,1,0:T(2,128)(2,1)}), bf16[8,2,1024]{2,1,0:T(2,128)(2,1)S(1)}, u32[]{:S(2)}, u32[]{:S(2)}) async-start(bf16[8,2,1024]{2,1,0:T(2,128)(2,1)} %copy.37), calls=%async_computation.3 | async-start | bytes 65536 | tf_op jit(solution)/shard_map/all_to_all | solution.py:118
  155.2 6.6 %all-to-all-done.2 = bf16[8,2,1024]{2,1,0:T(2,128)(2,1)S(1)} async-done(((bf16[8,2,1024]{2,1,0:T(2,128)(2,1)}), bf16[8,2,1024]{2,1,0:T(2,128)(2,1)S(1)}, u32[]{:S(2)}, u32[]{:S(2)}) %all-to-all-start.2) | async-done | bytes 32800 | tf_op jit(solution)/shard_map/all_to_all | solution.py:118
  161.8 0.7 fusion.17
  (40 shorter events, 3.3 us)
Async XLA Ops:
  6.5 42.9 %copy-start = (bf16[1024,512]{1,0:T(8,128)(2,1)S(1)}, bf16[1024,512]{1,0:T(8,128)(2,1)}, u32[]{:S(2)}) copy-start(bf16[1024,512]{1,0:T(8,128)(2,1)} %param.22) | copy-start | bytes 3145732
  50.4 12.2 %all-to-all-start = ((bf16[8,4,512]{2,1,0:T(4,128)(2,1)}), bf16[8,4,512]{2,1,0:T(4,128)(2,1)S(1)}, u32[]{:S(2)}, u32[]{:S(2)}) async-start(bf16[8,4,512]{2,1,0:T(4,128)(2,1)} %all_to_all.20), calls=%async_computation | async-start | bytes 65536 | tf_op jit(solution)/shard_map/all_to_all | solution.py:74
  55.8 34.5 %reduce-scatter.7.cloned.1.call-start = ((), (), s32[]{:S(2)}) async-start(), calls=%async_computation.6 | async-start | bytes 1310720
  64.0 84.2 %reduce-scatter.5.cloned.1.call-start = ((), (), s32[]{:S(2)}) async-start(), calls=%async_computation.5 | async-start | bytes 163840 | tf_op jit(solution)/shard_map/reduce_scatter | solution.py:115
  117.0 38.1 %copy-start.2 = (f32[4,2]{0,1:T(2,128)S(1)}, f32[4,2]{0,1:T(2,128)}, u32[]{:S(2)}) copy-start(f32[4,2]{0,1:T(2,128)} %param.25) | copy-start | bytes 100
  117.0 44.8 %copy-start.1 = (bf16[4,1024]{1,0:T(4,128)(2,1)S(1)}, bf16[4,1024]{1,0:T(4,128)(2,1)}, u32[]{:S(2)}) copy-start(bf16[4,1024]{1,0:T(4,128)(2,1)} %param.14) | copy-start | bytes 24580
  149.6 12.2 %all-to-all-start.2 = ((bf16[8,2,1024]{2,1,0:T(2,128)(2,1)}), bf16[8,2,1024]{2,1,0:T(2,128)(2,1)S(1)}, u32[]{:S(2)}, u32[]{:S(2)}) async-start(bf16[8,2,1024]{2,1,0:T(2,128)(2,1)} %copy.37), calls=%async_computation.3 | async-start | bytes 65536 | tf_op jit(solution)/shard_map/all_to_all | solution.py:118
Sparse Core Ops, SparseCore 0:
  64.1 26.1 reduce-scatter.6
  131.3 16.8 reduce-scatter.4
where the time goes:
time: 170 us; the launch traced here: 169 us
  blocking collectives  55.7 us (33%)
  waiting for transfers between devices  49.8 us (29%)
  matrix products  28.9 us (17%)
  between operations  13.6 us (8%)
  starting transfers between devices  11.1 us (7%)
  local copies, waits for them, and re-layouts  6.35 us (4%)
  other arithmetic  4 us (2%)
    all_gather x1, blocking collectives, shards(): every_row = lax.all_gather(attn_rows, 'dp', axis=0, tiled=True)  32.4 us
    unnamed x3, waiting for transfers between devices  26.2 us
    reduce_scatter x1, waiting for transfers between devices, shards(): lax.psum_scatter(slab_out.astype(jnp.bfloat16), 'head', scatter_dimension...  17 us
    all_to_all x1, blocking collectives, shards(): lax.all_to_all(outgoing, 'dp', split_axis=0, concat_axis=0, tiled=True)  12.8 us
    dot_general x1, matrix products, shards(): jnp.dot(hidden, w_down[0], preferred_element_type=jnp.float32)  7.82 us
    all_to_all x1, waiting for transfers between devices, shards(): lax.all_to_all(summed_total.astype(jnp.bfloat16), 'dp', split_axis=0, con...  6.6 us
    dot_general x1, matrix products, shards(): up_act = jnp.dot(flat_rows, w_in[0, 1], preferred_element_type=jnp.float32)  6.3 us
    dot_general x1, matrix products, shards(): jnp.dot(flat_rows, w_in[0, 0], preferred_element_type=jnp.float32)  6.24 us
  transfers between devices with their start and end apart: 4, of which 3 were waited for; matrix products, arithmetic and copies ran while one was open for 1% of the time, Pallas kernels for 0%

commit v1 on v0

--- a/solution.py
+++ b/solution.py
@@ -69,7 +69,15 @@
         + own_weight.astype(jnp.float32)[..., None] * value_new.astype(jnp.float32)[:, :, None, :]
     )
     attn_rows = attended.reshape(tok_rows, head_local * head_dim).astype(jnp.bfloat16)
-    every_row = lax.all_gather(attn_rows, "dp", axis=0, tiled=True)
+    every_row = jnp.concatenate(
+        jax.lax.all_to_all(
+            jnp.stack([attn_rows] * jax.lax.axis_size("dp")),
+            axis_name="dp",
+            split_axis=0,
+            concat_axis=0,
+        ),
+        axis=0,
+    )
     column_part = jnp.dot(every_row, w_out, preferred_element_type=jnp.float32)
     head_partial = lax.all_to_all(
         column_part.astype(jnp.bfloat16), "dp", split_axis=0, concat_axis=1, tiled=True

time: 170 us -> 149 us (0.88)
  blocking collectives: 55.7 us -> 23.4 us
  waiting for transfers between devices: 49.8 us -> 55.4 us
  starting transfers between devices: 11.1 us -> 16.2 us
    all_gather x1 -> x0, blocking collectives: 32.4 us -> none  [shards(): every_row = lax.all_gather(attn_rows, 'dp', axis=0, tiled=True)]
    all_to_all x0 -> x1, starting transfers between devices: none -> 7.28 us  [shards(): jax.lax.all_to_all(jnp.stack([attn_rows] * jax.lax.axis_size('dp')), axis...]
    all_to_all x0 -> x1, waiting for transfers between devices: none -> 5.68 us  [shards(): jax.lax.all_to_all(jnp.stack([attn_rows] * jax.lax.axis_size('dp')), axis...]
    all_to_all x1, starting transfers between devices: 5.46 us -> 3.33 us  [shards(): lax.all_to_all(column_part.astype(jnp.bfloat16), 'dp', split_axis=0, conc...]
  transfers between devices with their start and end apart: 4 -> 5, of which waited for: 3 -> 5; matrix products, arithmetic and copies ran while one was open for 1% -> 1% of each run, Pallas kernels for 0% -> 0%
where the time goes in v1:
time: 149 us; the launch traced here: 148 us
  waiting for transfers between devices  55.4 us (37%)
  matrix products  28.9 us (19%)
  blocking collectives  23.4 us (16%)
  starting transfers between devices  16.2 us (11%)
  between operations  13.6 us (9%)
  local copies, waits for them, and re-layouts  6.99 us (5%)
  other arithmetic  4 us (3%)
    unnamed x3, waiting for transfers between devices  25 us
    reduce_scatter x1, waiting for transfers between devices, shards(): lax.psum_scatter(slab_out.astype(jnp.bfloat16), 'head', scatter_dimension...  17 us
    all_to_all x1, blocking collectives, shards(): lax.all_to_all(outgoing, 'dp', split_axis=0, concat_axis=0, tiled=True)  12.8 us
    dot_general x1, matrix products, shards(): jnp.dot(hidden, w_down[0], preferred_element_type=jnp.float32)  7.82 us
    all_to_all x1, starting transfers between devices, shards(): jax.lax.all_to_all(jnp.stack([attn_rows] * jax.lax.axis_size('dp')), axis...  7.28 us
    all_to_all x1, waiting for transfers between devices, shards(): lax.all_to_all(summed_total.astype(jnp.bfloat16), 'dp', split_axis=0, con...  6.6 us
    dot_general x1, matrix products, shards(): up_act = jnp.dot(flat_rows, w_in[0, 1], preferred_element_type=jnp.float32)  6.3 us
    dot_general x1, matrix products, shards(): jnp.dot(flat_rows, w_in[0, 0], preferred_element_type=jnp.float32)  6.24 us
  transfers between devices with their start and end apart: 5, of which 5 were waited for; matrix products, arithmetic and copies ran while one was open for 1% of the time, Pallas kernels for 0%

profile of v1, /device:TPU:0, one launch (start us, length us, event | category | flops | bytes accessed | tf_op | source)
XLA Modules:
  0.0 148.4 jit_solution(14691631741744496155)
XLA Ops:
  6.5 0.9 fusion.19
  8.0 0.7 iota_compare_fusion.1
  8.8 0.8 fusion.30
  9.6 3.5 %select_reduce_fusion = (f32[4,2,4]{2,1,0:T(2,128)S(1)}, f32[4,2,4,2048]{3,2,1,0:T(4,128)S(1)}) fusion(pred[4,2,2048]{2,1,0:T(4,128)(4,1)S(1)} %copy.32, bf16[4,2,4,128]{3,2,1,0:T(4,128)(2,1)} %bitcast.52, bf16[4,2,2048,128]{3,2,1,0:T(8,128)(2,1)} %param.18), kind=kOutput, calls=%fused_computation.19 | convolution fusion | flops 16973792 | bytes 4481152 | tf_op jit(solution)/shard_map/bkgd,bksd->bkgs/dot_general | solution.py:48
  14.1 2.9 %fusion.18 = bf16[4,2,4,128]{3,2,1,0:T(4,128)(2,1)S(1)} fusion(bf16[4,2,2048,128]{3,2,1,0:T(8,128)(2,1)} %param.19, f32[4,2,4,2048]{3,2,1,0:T(4,128)S(1)} %get-tuple-element.8, f32[4,2,4]{2,1,0:T(2,128)S(1)} %get-tuple-element.6, f32[4,2,4]{2,1,0:T(2,128)S(1)} %multiply_maximum_fusion, pred[4,2,2048]{2,1,0:T(4,128)(4,1)S(1)} %copy.32, ...), kind=kOutput, calls=%fused_computation.17 | convolution fusion | flops 17051648 | bytes 4485504 | tf_op jit(solution)/shard_map/bkgs,bksd->bkgd/dot_general | solution.py:64
  17.7 7.3 %all-to-all-start = ((bf16[8,4,1024]{2,1,0:T(4,128)(2,1)}), bf16[8,4,1024]{2,1,0:T(4,128)(2,1)S(1)}, u32[]{:S(2)}, u32[]{:S(2)}) async-start(bf16[8,4,1024]{2,1,0:T(4,128)(2,1)} %stack.2), calls=%async_computation | async-start | bytes 131072 | tf_op jit(solution)/shard_map/all_to_all | solution.py:73
  25.0 0.8 copy.33
  26.2 5.7 %all-to-all-done = bf16[8,4,1024]{2,1,0:T(4,128)(2,1)S(1)} async-done(((bf16[8,4,1024]{2,1,0:T(4,128)(2,1)}), bf16[8,4,1024]{2,1,0:T(4,128)(2,1)S(1)}, u32[]{:S(2)}, u32[]{:S(2)}) %all-to-all-start) | async-done | bytes 65568 | tf_op jit(solution)/shard_map/all_to_all | solution.py:73
  32.9 3.3 %all-to-all-start.1 = ((bf16[8,4,512]{2,1,0:T(4,128)(2,1)}), bf16[8,4,512]{2,1,0:T(4,128)(2,1)S(1)}, u32[]{:S(2)}, u32[]{:S(2)}) async-start(bf16[8,4,512]{2,1,0:T(4,128)(2,1)} %all_to_all.24), calls=%async_computation.1 | async-start | bytes 65536 | tf_op jit(solution)/shard_map/all_to_all | solution.py:82
  36.4 5.3 %all_gather.7 = f32[4096]{0:T(1024)S(1)} all-gather(f32[1024]{0:T(1024)} %param.23), channel_id=1, replica_groups=mesh['dp'=8,'head'=4] {'head'}, dimensions={0}, use_global_device_ids=true | all-gather | bytes 20480 | tf_op jit(solution)/shard_map/all_gather | solution.py:90
  41.7 1.1 all-to-all-done.1
  42.8 1.4 copy.40
  44.4 25.0 %reduce-scatter.7.cloned.1.call-done = bf16[1024,4]{1,0:T(8,128)(2,1)} async-done(((bf16[4096,4]{1,0:T(8,128)(2,1)}), bf16[1024,4]{1,0:T(8,128)(2,1)}) %reduce-scatter.7.cloned.1.call-update) | async-done | bytes 8208
  69.4 1.1 copy.41
  71.2 5.2 %all_gather.6 = f32[4,4096]{1,0:T(4,128)S(1)} all-gather(f32[4,1024]{1,0:T(4,128)S(1)} %convert_add_fusion), channel_id=1, replica_groups=mesh['dp'=8,'head'=4] {'head'}, dimensions={1}, use_global_device_ids=true | all-gather | bytes 81920 | tf_op jit(solution)/shard_map/all_gather | solution.py:89
  76.9 12.8 %all_to_all.34 = bf16[8,2,4096]{2,1,0:T(2,128)(2,1)S(1)} all-to-all(bf16[8,2,4096]{2,1,0:T(2,128)(2,1)S(1)} %reshape_reshape.3), channel_id=1, replica_groups=mesh['dp'=8,'head'=4] {'dp'}, dimensions={0} | all-to-all | bytes 262144 | tf_op jit(solution)/shard_map/all_to_all | solution.py:114
  89.8 6.2 %fusion.4 = f32[16,1792]{1,0:T(8,128)S(1)} fusion(bf16[16,4096]{1,0:T(8,128)(2,1)S(1)} %reshape.104, bf16[1,2,4096,1792]{3,2,1,0:T(8,128)(2,1)} %param.26), kind=kOutput, calls=%fused_computation.4 | convolution fusion | flops 234881024 | bytes 14925824 | tf_op jit(solution)/shard_map/dot_general | solution.py:117
  96.1 6.3 %fusion.14 = bf16[16,1792]{1,0:T(8,128)(2,1)S(1)} fusion(bf16[16,4096]{1,0:T(8,128)(2,1)S(1)} %reshape.104, bf16[1,2,4096,1792]{3,2,1,0:T(8,128)(2,1)} %param.26, f32[16,1792]{1,0:T(8,128)S(1)} %fusion.4), kind=kOutput, calls=%fused_computation.12 | convolution fusion | flops 235053056 | bytes 14983168 | tf_op jit(solution)/shard_map/dot_general | solution.py:118
  102.4 7.8 %fusion.8 = bf16[8,2,4096]{2,0,1:T(8,128)(2,1)} fusion(bf16[1,1792,4096]{2,1,0:T(8,128)(2,1)} %param.27, bf16[8,2,1792]{2,1,0:T(2,128)(2,1)S(1)} %dot_general.36), kind=kOutput, calls=%fused_computation.8 | convolution fusion | flops 234946560 | bytes 14868480 | tf_op jit(solution)/shard_map/dot_general | solution.py:120
  110.2 17.0 %reduce-scatter.5.cloned.1.call-done = bf16[8,2,1024]{2,0,1:T(8,128)(2,1)} async-done(((bf16[8,2,4096]{2,0,1:T(8,128)(2,1)}), bf16[8,2,1024]{2,0,1:T(8,128)(2,1)}) %reduce-scatter.5.cloned.1.call-update) | async-done | bytes 32784 | tf_op jit(solution)/shard_map/reduce_scatter | solution.py:123
  127.2 1.4 copy.37
  128.6 5.5 %all-to-all-start.3 = ((bf16[8,2,1024]{2,1,0:T(2,128)(2,1)}), bf16[8,2,1024]{2,1,0:T(2,128)(2,1)S(1)}, u32[]{:S(2)}, u32[]{:S(2)}) async-start(bf16[8,2,1024]{2,1,0:T(2,128)(2,1)} %copy.37), calls=%async_computation.4 | async-start | bytes 65536 | tf_op jit(solution)/shard_map/all_to_all | solution.py:126
  134.2 6.6 %all-to-all-done.3 = bf16[8,2,1024]{2,1,0:T(2,128)(2,1)S(1)} async-done(((bf16[8,2,1024]{2,1,0:T(2,128)(2,1)}), bf16[8,2,1024]{2,1,0:T(2,128)(2,1)S(1)}, u32[]{:S(2)}, u32[]{:S(2)}) %all-to-all-start.3) | async-done | bytes 32800 | tf_op jit(solution)/shard_map/all_to_all | solution.py:126
  140.9 0.7 fusion.17
  (42 shorter events, 5.3 us)
Async XLA Ops:
  6.5 25.4 %copy-start = (bf16[1024,512]{1,0:T(8,128)(2,1)S(1)}, bf16[1024,512]{1,0:T(8,128)(2,1)}, u32[]{:S(2)}) copy-start(bf16[1024,512]{1,0:T(8,128)(2,1)} %param.22) | copy-start | bytes 3145732
  17.7 14.2 %all-to-all-start = ((bf16[8,4,1024]{2,1,0:T(4,128)(2,1)}), bf16[8,4,1024]{2,1,0:T(4,128)(2,1)S(1)}, u32[]{:S(2)}, u32[]{:S(2)}) async-start(bf16[8,4,1024]{2,1,0:T(4,128)(2,1)} %stack.2), calls=%async_computation | async-start | bytes 131072 | tf_op jit(solution)/shard_map/all_to_all | solution.py:73
  32.9 10.0 %all-to-all-start.1 = ((bf16[8,4,512]{2,1,0:T(4,128)(2,1)}), bf16[8,4,512]{2,1,0:T(4,128)(2,1)S(1)}, u32[]{:S(2)}, u32[]{:S(2)}) async-start(bf16[8,4,512]{2,1,0:T(4,128)(2,1)} %all_to_all.24), calls=%async_computation.1 | async-start | bytes 65536 | tf_op jit(solution)/shard_map/all_to_all | solution.py:82
  36.2 33.2 %reduce-scatter.7.cloned.1.call-start = ((), (), s32[]{:S(2)}) async-start(), calls=%async_computation.7 | async-start | bytes 1310720
  44.3 83.0 %reduce-scatter.5.cloned.1.call-start = ((), (), s32[]{:S(2)}) async-start(), calls=%async_computation.6 | async-start | bytes 163840 | tf_op jit(solution)/shard_map/reduce_scatter | solution.py:123
  96.0 38.1 %copy-start.2 = (f32[4,2]{0,1:T(2,128)S(1)}, f32[4,2]{0,1:T(2,128)}, u32[]{:S(2)}) copy-start(f32[4,2]{0,1:T(2,128)} %param.25) | copy-start | bytes 100
  96.0 44.8 %copy-start.1 = (bf16[4,1024]{1,0:T(4,128)(2,1)S(1)}, bf16[4,1024]{1,0:T(4,128)(2,1)}, u32[]{:S(2)}) copy-start(bf16[4,1024]{1,0:T(4,128)(2,1)} %param.14) | copy-start | bytes 24580
  128.6 12.2 %all-to-all-start.3 = ((bf16[8,2,1024]{2,1,0:T(2,128)(2,1)}), bf16[8,2,1024]{2,1,0:T(2,128)(2,1)S(1)}, u32[]{:S(2)}, u32[]{:S(2)}) async-start(bf16[8,2,1024]{2,1,0:T(2,128)(2,1)} %copy.37), calls=%async_computation.4 | async-start | bytes 65536 | tf_op jit(solution)/shard_map/all_to_all | solution.py:126
Sparse Core Ops, SparseCore 0:
  44.4 24.9 reduce-scatter.6
  110.4 16.8 reduce-scatter.4
